TPU v7x, 256 devices: a whole 4x4x8 slice. The times are simulated.
256 devices in a mesh: tok: 8 (over z), tp: 16 (over y, x), grp: 2 (over core).
Axes of the slice: x: 4, y: 4, z: 8, core: 2. Of those that a mesh axis runs over, the one named last changes fastest.
Arguments:
- hidden: bfloat16 [2048, 6144], P(('tok', 'grp'), 'tp'), may hold values from -6 to 6
- gain: bfloat16 [6144], P('tp'), may hold values from 0.5 to 1.5
- expert_ids: int32 [2048, 2], P(('tok', 'grp')), may hold values from 0 to 7, all different within a row; in each aligned block of 128 rows (0 to 127, 128 to 255, ...) at most 40 rows name the same one
- gate_weights: float32 [2048, 2], P(('tok', 'grp')), may hold values from 0.1 to 0.9
- segment_ids: int32 [2048], P(('tok', 'grp')), may hold values from 0 to 15, never falling along the last dimension, each value on 1 to 384 neighbouring positions
- upstream: bfloat16 [2048, 6144], P(('tok', 'grp'), 'tp'), may hold values from -6 to 6
- w_gate: bfloat16 [8, 6144, 8192], P('tok', None, ('tp', 'grp')), may hold values from -0.078125 to 0.078125
- w_up: bfloat16 [8, 6144, 8192], P('tok', None, ('tp', 'grp')), may hold values from -0.078125 to 0.078125
- w_down: bfloat16 [8, 8192, 6144], P('tok', ('tp', 'grp')), may hold values from -0.0625 to 0.0625
Outputs:
- mixed: bfloat16 [2048, 6144], P(('tok', 'grp'), 'tp')
- importance: float32 [8, 8192], P('tok', ('tp', 'grp'))
Inputs may be any that keep to these rules, and one draw needn't show every extreme that they name: `expert_ids`: each token names 2 different experts. Within the tokens of one token shard (aligned blocks of 128 rows) no expert is named by more than 40 tokens, and in some block one expert is named by exactly 40. `segment_ids`: never falling along the tokens; every document holds between 1 and 384 tokens.
All inputs are finite; a program needn't handle non-finite values.
Results may differ from a plain program's by a relative error of at most 0.0095.
Values may be sent and summed in bfloat16 or wider, within the bound.
No kernel may reach another device: no remote copies, remote signals or barrier semaphores. Data moves between devices by JAX's collectives and lax.ppermute only.
A program may use at most 128 MiB of HBM per device.

v0:
```python
import jax
import jax.numpy as jnp
from jax import lax
from jax.sharding import PartitionSpec as P


def expert_pass(rows_in, cot_in, gate_mat, up_mat, down_mat):
    gate_pre = jnp.dot(rows_in, gate_mat, preferred_element_type=jnp.float32)
    up_proj = jnp.dot(rows_in, up_mat, preferred_element_type=jnp.float32)
    sigmoid_gate = jax.nn.sigmoid(gate_pre)
    activated = gate_pre * sigmoid_gate
    hidden_act = (activated * up_proj).astype(jnp.bfloat16)
    grad_act = lax.dot_general(
        cot_in, down_mat, (((1,), (1,)), ((), ())), preferred_element_type=jnp.float32
    )
    grad_gate = (
        grad_act * up_proj * sigmoid_gate * (1.0 + gate_pre * (1.0 - sigmoid_gate))
    ).astype(jnp.bfloat16)
    grad_up = (grad_act * activated).astype(jnp.bfloat16)
    grad_wgate = lax.dot_general(
        rows_in, grad_gate, (((0,), (0,)), ((), ())), preferred_element_type=jnp.float32
    )
    grad_wup = lax.dot_general(
        rows_in, grad_up, (((0,), (0,)), ((), ())), preferred_element_type=jnp.float32
    )
    grad_wdown = lax.dot_general(
        hidden_act, cot_in, (((0,), (0,)), ((), ())), preferred_element_type=jnp.float32
    )
    scores = jnp.sum(jnp.abs(grad_wgate * gate_mat.astype(jnp.float32)), axis=0)
    scores = scores + jnp.sum(jnp.abs(grad_wup * up_mat.astype(jnp.float32)), axis=0)
    scores = scores + jnp.sum(jnp.abs(grad_wdown * down_mat.astype(jnp.float32)), axis=1)
    return (hidden_act, scores)


def on_device(hidden, gain, expert_ids, gate_weights, segment_ids, upstream, w_gate, w_up, w_down):
    rows_here = hidden.shape[0]
    top_count = expert_ids.shape[1]
    experts = lax.axis_size("tok")
    groups = lax.axis_size("grp")
    capacity = 5 * rows_here // (2 * experts)
    width = w_gate.shape[1]
    documents = jnp.arange(experts * groups, dtype=jnp.int32)
    doc_onehot = (segment_ids[:, None] == documents[None, :]).astype(jnp.float32)
    doc_len = lax.psum(jnp.sum(doc_onehot, axis=0), ("tok", "grp"))
    tok_len = jnp.sum(doc_onehot * doc_len[None, :], axis=1)
    tok_weight = rows_here / tok_len
    onehot = (
        expert_ids.reshape(-1)[:, None] == jnp.arange(experts, dtype=jnp.int32)[None, :]
    ).astype(jnp.int32)
    before = jnp.cumsum(onehot, axis=0) - onehot
    slot_ids = jnp.sum(before * onehot, axis=1).reshape(rows_here, top_count)
    targets = expert_ids * capacity + slot_ids
    all_slots = jnp.arange(experts * capacity, dtype=jnp.int32)
    matches = all_slots[:, None, None] == targets[None, :, :]
    placing = jnp.any(matches, axis=2).astype(jnp.bfloat16)
    scaled = gate_weights * tok_weight[:, None]
    slot_scale = jnp.sum(jnp.where(matches, scaled[None, :, :], 0.0), axis=(1, 2))
    combining = jnp.sum(jnp.where(matches, gate_weights[None, :, :], 0.0), axis=2)
    wide_hidden = hidden.astype(jnp.float32)
    squares = lax.psum(jnp.sum(wide_hidden * wide_hidden, axis=1), "tp")
    scaling = lax.rsqrt(squares / width + 1e-05)
    normed = (wide_hidden * scaling[:, None] * gain.astype(jnp.float32)[None, :]).astype(
        jnp.bfloat16
    )
    block_rows = jnp.dot(placing, normed, preferred_element_type=jnp.float32).astype(jnp.bfloat16)
    block_cot = jnp.dot(placing, upstream, preferred_element_type=jnp.float32) * slot_scale[:, None]
    block_rows = block_rows.reshape(experts, capacity, -1)
    block_cot = block_cot.astype(jnp.bfloat16).reshape(experts, capacity, -1)
    came_rows, came_cot = (
        lax.all_to_all(block_rows, "tok", split_axis=0, concat_axis=0, tiled=True),
        lax.all_to_all(block_cot, "tok", split_axis=0, concat_axis=0, tiled=True),
    )
    part_rows, part_cot = (
        lax.all_gather(came_rows, "tp", axis=2, tiled=True),
        lax.all_gather(came_cot, "tp", axis=2, tiled=True),
    )
    pooled_rows, pooled_cot = (
        lax.all_gather(part_rows, "grp", axis=0, tiled=True),
        lax.all_gather(part_cot, "grp", axis=0, tiled=True),
    )
    rows_in = pooled_rows.reshape(-1, width)
    cot_in = pooled_cot.reshape(-1, width)
    gate_mat = w_gate[0]
    up_mat = w_up[0]
    down_mat = w_down[0]
    hidden_act, scores = expert_pass(rows_in, cot_in, gate_mat, up_mat, down_mat)
    importance = scores / (rows_here * experts * groups)
    partial_value = lax.psum_scatter(
        lax.dot_general(
            down_mat, hidden_act, (((0,), (1,)), ((), ())), preferred_element_type=jnp.float32
        ).astype(jnp.bfloat16),
        "tp",
        scatter_dimension=0,
        tiled=True,
    )
    summed = lax.psum_scatter(partial_value, "grp", scatter_dimension=1, tiled=True).astype(
        jnp.float32
    )
    slice_width = summed.shape[0]
    outgoing = summed.astype(jnp.bfloat16).reshape(slice_width, experts, capacity)
    returned = lax.all_to_all(outgoing, "tok", split_axis=1, concat_axis=1, tiled=True)
    returned = returned.reshape(slice_width, experts * capacity).astype(jnp.float32)
    combined = lax.dot_general(
        combining,
        returned,
        (((0,), (1,)), ((), ())),
        precision=lax.Precision.HIGHEST,
        preferred_element_type=jnp.float32,
    )
    mixed = (hidden.astype(jnp.float32) + combined).astype(jnp.bfloat16)
    return (mixed, importance[None, :])


def solution(mesh):
    placed = (
        P(("tok", "grp"), "tp"),
        P("tp"),
        P(("tok", "grp"), None),
        P(("tok", "grp"), None),
        P(("tok", "grp")),
        P(("tok", "grp"), "tp"),
        P("tok", None, ("tp", "grp")),
        P("tok", None, ("tp", "grp")),
        P("tok", ("tp", "grp"), None),
    )
    return jax.shard_map(
        on_device,
        mesh=mesh,
        in_specs=placed,
        out_specs=(P(("tok", "grp"), "tp"), P("tok", ("tp", "grp"))),
        check_vma=False,
    )
```

profile of v0, /device:TPU:1, one launch (start us, length us, event | category | flops | bytes accessed | tf_op | source)
XLA Modules:
  0.0 378.7 jit_solution(2218602018310981666)
XLA Ops:
  8.5 1.0 fusion.19
  9.5 34.2 %psum.14 = f32[128]{0:T(128)S(1)} all-reduce(f32[128]{0:T(128)S(1)} %fusion.19), channel_id=1, replica_groups=mesh['tok'=8,'tp'=16,'grp'=2] {'tp'}, use_global_device_ids=true, to_apply=%region_6.7 | all-reduce | flops 128 | bytes 1024 | tf_op jit(solution)/shard_map/psum | solution.py:60
  46.3 1.2 convolution_convert_fusion.1
  47.5 17.2 %all_to_all.15 = bf16[8,40,384]{2,1,0:T(8,128)(2,1)} all-to-all(bf16[8,40,384]{2,1,0:T(8,128)(2,1)S(1)} %bitcast.56), channel_id=1, replica_groups=mesh['tok'=8,'tp'=16,'grp'=2] {'tok'}, dimensions={0} | all-to-all | bytes 491520 | tf_op jit(solution)/shard_map/all_to_all | solution.py:70
  65.6 32.2 %psum.15 = f32[16]{0:T(128)S(1)} all-reduce(f32[16]{0:T(128)S(1)} %convert_reduce_fusion), channel_id=1, replica_groups=mesh['tok'=8,'tp'=16,'grp'=2] {'tok','grp'}, use_global_device_ids=true, to_apply=%region_10.11 | all-reduce | flops 16 | bytes 128 | tf_op jit(solution)/shard_map/psum | solution.py:44
  99.2 1.5 select_reduce_fusion
  101.0 12.8 %all_to_all.16 = bf16[8,40,384]{2,1,0:T(8,128)(2,1)} all-to-all(bf16[8,40,384]{2,1,0:T(8,128)(2,1)S(1)} %bitcast.57), channel_id=1, replica_groups=mesh['tok'=8,'tp'=16,'grp'=2] {'tok'}, dimensions={0} | all-to-all | bytes 491520 | tf_op jit(solution)/shard_map/all_to_all | solution.py:71
  113.8 10.2 %all-gather.5.cloned.1.call-done = bf16[8,40,6144]{2,1,0:T(8,128)(2,1)} async-done(((bf16[8,40,384]{2,1,0:T(8,128)(2,1)}), bf16[8,40,6144]{2,1,0:T(8,128)(2,1)}) %all-gather.5.cloned.1.call-update) | async-done | bytes 3932176 | tf_op jit(solution)/shard_map/all_gather | solution.py:74
  124.1 62.4 %all-gather.9.cloned.1.call-done = bf16[8,40,6144]{2,1,0:T(8,128)(2,1)} async-done(((bf16[8,40,384]{2,1,0:T(8,128)(2,1)}), bf16[8,40,6144]{2,1,0:T(8,128)(2,1)}) %all-gather.9.cloned.1.call-update) | async-done | bytes 3932176 | tf_op jit(solution)/shard_map/all_gather | solution.py:75
  186.5 27.7 %all-gather.7.cloned.1.call-done = bf16[16,40,6144]{2,1,0:T(8,128)(2,1)} async-done(((bf16[8,40,6144]{2,1,0:T(8,128)(2,1)}), bf16[16,40,6144]{2,1,0:T(8,128)(2,1)}) %all-gather.7.cloned.1.call-update) | async-done | bytes 7864336 | tf_op jit(solution)/shard_map/all_gather | solution.py:78
  214.2 5.6 %fusion.9 = f32[640,256]{1,0:T(8,128)S(1)} fusion(bf16[640,6144]{1,0:T(8,128)(2,1)} %bitcast.60, bf16[1,6144,256]{2,1,0:T(8,128)(2,1)S(1)} %copy-done.4), kind=kOutput, calls=%fused_computation.13 | convolution fusion | flops 2013265920 | bytes 11665408 | tf_op jit(solution)/shard_map/dot_general | solution.py:8
  220.6 3.0 multiply_convert_fusion.2
  224.4 6.1 %fusion = bf16[6144,640]{0,1:T(8,128)(2,1)} fusion(bf16[640,256]{1,0:T(8,128)(2,1)S(1)} %get-tuple-element.4, bf16[1,256,6144]{2,1,0:T(8,128)(2,1)S(1)} %copy-done.1), kind=kOutput, calls=%fused_computation.1 | convolution fusion | flops 2017198080 | bytes 11337728 | tf_op jit(solution)/shard_map/dot_general | solution.py:89
  230.5 10.7 %copy.34 = bf16[6144,640]{1,0:T(8,128)(2,1)} copy(bf16[6144,640]{0,1:T(8,128)(2,1)} %fusion) | data formatting | bytes 15728640
  241.6 5.6 %fusion.4 = f32[640,256]{1,0:T(8,128)S(1)} fusion(bf16[640,6144]{1,0:T(8,128)(2,1)} %bitcast.53, bf16[1,256,6144]{2,1,0:T(8,128)(2,1)S(1)} %copy-done.1), kind=kOutput, calls=%fused_computation.8 | convolution fusion | flops 2013265920 | bytes 11665408 | tf_op jit(solution)/shard_map/dot_general | solution.py:13
  248.1 6.2 %fusion.11 = f32[256]{0:T(256)S(1)} fusion(bf16[1,6144,256]{2,1,0:T(8,128)(2,1)S(1)} %copy-done.5, bf16[640,6144]{1,0:T(8,128)(2,1)} %bitcast.61, f32[640,256]{1,0:T(8,128)S(1)} %copy-done.8, f32[640,256]{1,0:T(8,128)S(1)} %fusion.4, f32[640,256]{1,0:T(8,128)S(1)} %copy-done.10), kind=kOutput, calls=%fused_computation.15 | convolution fusion | flops 2021195520 | bytes 12977152 | tf_op jit(solution)/shard_map/dot_general | solution.py:20
  254.3 80.1 %reduce-scatter.7.cloned.1.call-done = bf16[384,640]{1,0:T(8,128)(2,1)} async-done(((bf16[6144,640]{1,0:T(8,128)(2,1)}), bf16[384,640]{1,0:T(8,128)(2,1)}) %reduce-scatter.7.cloned.1.call-update) | async-done | bytes 491536
  334.4 2.0 copy.35
  336.5 7.4 %fusion.12 = f32[256]{0:T(256)S(1)} fusion(bf16[1,6144,256]{2,1,0:T(8,128)(2,1)} %param.16, bf16[640,6144]{1,0:T(8,128)(2,1)} %bitcast.62, f32[640,256]{1,0:T(8,128)} %copy-done.9, f32[640,256]{1,0:T(8,128)} %copy-done.7), kind=kOutput, calls=%fused_computation.16 | convolution fusion | flops 2020540160 | bytes 12321792 | tf_op jit(solution)/shard_map/dot_general | solution.py:23
  343.8 7.7 %reduce-scatter.5.cloned.1.call-done = bf16[384,320]{0,1:T(8,128)(2,1)} async-done(((bf16[384,640]{0,1:T(8,128)(2,1)}), bf16[384,320]{0,1:T(8,128)(2,1)}) %reduce-scatter.5.cloned.1.call-update) | async-done | bytes 245776 | tf_op jit(solution)/shard_map/reduce_scatter | solution.py:96
  351.5 6.5 %all-to-all-start.1 = ((bf16[384,8,40]{0,2,1:T(8,128)(2,1)}), bf16[384,8,40]{0,2,1:T(8,128)(2,1)S(1)}, u32[]{:S(2)}, u32[]{:S(2)}) async-start(bf16[384,8,40]{0,2,1:T(8,128)(2,1)} %bitcast.58), calls=%async_computation.2 | async-start | bytes 491520 | tf_op jit(solution)/shard_map/all_to_all | solution.py:101
  358.0 6.5 %fusion.13 = f32[256]{0:T(256)S(1)} fusion(bf16[1,256,6144]{2,1,0:T(8,128)(2,1)S(1)} %copy-done.1, bf16[640,256]{1,0:T(8,128)(2,1)} %copy-done.2, bf16[640,6144]{1,0:T(8,128)(2,1)} %bitcast.54), kind=kOutput, calls=%fused_computation.17 | convolution fusion | flops 2019557120 | bytes 11338752 | tf_op jit(solution)/shard_map/dot_general | solution.py:26
  365.0 4.8 %all-to-all-done.1 = bf16[384,8,40]{0,2,1:T(8,128)(2,1)S(1)} async-done(((bf16[384,8,40]{0,2,1:T(8,128)(2,1)}), bf16[384,8,40]{0,2,1:T(8,128)(2,1)S(1)}, u32[]{:S(2)}, u32[]{:S(2)}) %all-to-all-start.1) | async-done | bytes 245792 | tf_op jit(solution)/shard_map/all_to_all | solution.py:101
  369.8 2.0 fusion.15
  (56 shorter events, 9.8 us)
Async XLA Ops:
  7.2 93.6 %copy-start = (bf16[128,384]{1,0:T(8,128)(2,1)S(1)}, bf16[128,384]{1,0:T(8,128)(2,1)}, u32[]{:S(2)}) copy-start(bf16[128,384]{1,0:T(8,128)(2,1)} %param.14) | copy-start | bytes 294916
  7.2 207.0 %copy-start.4 = (bf16[1,6144,256]{2,1,0:T(8,128)(2,1)S(1)}, bf16[1,6144,256]{2,1,0:T(8,128)(2,1)}, u32[]{:S(2)}) copy-start(bf16[1,6144,256]{2,1,0:T(8,128)(2,1)} %param.15) | copy-start | bytes 9437188
  7.2 116.8 %all-gather.5.cloned.1.call-start = ((), (), s32[]{:S(2)}) async-start(), calls=%async_computation.5 | async-start | bytes 4177920 | tf_op jit(solution)/shard_map/all_gather | solution.py:74
  64.7 121.7 %all-gather.9.cloned.1.call-start = ((), (), s32[]{:S(2)}) async-start(), calls=%async_computation.8 | async-start | bytes 4177920 | tf_op jit(solution)/shard_map/all_gather | solution.py:75
  113.8 100.4 %all-gather.7.cloned.1.call-start = ((), (), s32[]{:S(2)}) async-start(), calls=%async_computation.6 | async-start | bytes 11796480 | tf_op jit(solution)/shard_map/all_gather | solution.py:78
  124.1 117.6 %all-gather.11.cloned.1.call-start = ((), (), s32[]{:S(2)}) async-start(), calls=%async_computation.9 | async-start | bytes 11796480 | tf_op jit(solution)/shard_map/all_gather | solution.py:79
  186.5 147.9 %reduce-scatter.7.cloned.1.call-start = ((), (), s32[]{:S(2)}) async-start(), calls=%async_computation.10 | async-start | bytes 8355840
  214.2 5.6 %copy-start.3 = (bf16[16,40,6144]{2,1,0:T(8,128)(2,1)S(1)}, bf16[16,40,6144]{2,1,0:T(8,128)(2,1)}, u32[]{:S(2)}) copy-start(bf16[16,40,6144]{2,1,0:T(8,128)(2,1)} %all-gather.7.cloned.1.call-done) | copy-start | bytes 23592964
  214.2 6.4 %copy-start.6 = (bf16[1,6144,256]{2,1,0:T(8,128)(2,1)S(1)}, bf16[1,6144,256]{2,1,0:T(8,128)(2,1)}, u32[]{:S(2)}) copy-start(bf16[1,6144,256]{2,1,0:T(8,128)(2,1)} %param.16) | copy-start | bytes 9437188
  220.6 3.0 copy-start.7
  220.6 3.8 copy-start.1
  223.6 0.7 copy-start.2
  241.2 110.2 %reduce-scatter.5.cloned.1.call-start = ((), (), s32[]{:S(2)}) async-start(), calls=%async_computation.7 | async-start | bytes 737280 | tf_op jit(solution)/shard_map/reduce_scatter | solution.py:96
  241.6 6.5 %copy-start.5 = (bf16[1,6144,256]{2,1,0:T(8,128)(2,1)S(1)}, bf16[1,6144,256]{2,1,0:T(8,128)(2,1)}, u32[]{:S(2)}) copy-start(bf16[1,6144,256]{2,1,0:T(8,128)(2,1)} %param.15) | copy-start | bytes 9437188
  241.6 6.5 %copy-start.8 = (f32[640,256]{1,0:T(8,128)S(1)}, f32[640,256]{1,0:T(8,128)}, u32[]{:S(2)}) copy-start(f32[640,256]{1,0:T(8,128)} %copy-done.7) | copy-start | bytes 1966084
  241.6 6.5 %copy-start.10 = (f32[640,256]{1,0:T(8,128)S(1)}, f32[640,256]{1,0:T(8,128)}, u32[]{:S(2)}) copy-start(f32[640,256]{1,0:T(8,128)} %get-tuple-element.5) | copy-start | bytes 1966084
  247.2 0.8 copy-start.9
  351.5 18.3 %all-to-all-start.1 = ((bf16[384,8,40]{0,2,1:T(8,128)(2,1)}), bf16[384,8,40]{0,2,1:T(8,128)(2,1)S(1)}, u32[]{:S(2)}, u32[]{:S(2)}) async-start(bf16[384,8,40]{0,2,1:T(8,128)(2,1)} %bitcast.58), calls=%async_computation.2 | async-start | bytes 491520 | tf_op jit(solution)/shard_map/all_to_all | solution.py:101
Sparse Core Ops, SparseCore 0:
  64.9 59.1 all-gather.4
  126.4 59.9 all-gather.8
  188.3 25.9 all-gather.6
  215.9 25.6 all-gather.10
  245.3 89.1 reduce-scatter.6
  336.8 14.6 reduce-scatter.4
where the time goes:
time: 379 us
  waiting for transfers between devices  193 us (51%)
  blocking collectives  96.5 us (25%)
  matrix products  43.9 us (12%)
  local copies, waits for them, and re-layouts  16.8 us (4%)
  between operations  14.2 us (4%)
  other arithmetic  7.42 us (2%)
  starting transfers between devices  6.89 us (2%)
    unnamed x7, waiting for transfers between devices  80.2 us
    all_gather x1, waiting for transfers between devices, on_device(): lax.all_gather(came_cot, 'tp', axis=2, tiled=True)  62.4 us
    psum x1, blocking collectives, on_device(): squares = lax.psum(jnp.sum(wide_hidden * wide_hidden, axis=1), 'tp')  34.2 us
    psum x1, blocking collectives, on_device(): doc_len = lax.psum(jnp.sum(doc_onehot, axis=0), ('tok', 'grp'))  32.2 us
    all_gather x1, waiting for transfers between devices, on_device(): lax.all_gather(part_rows, 'grp', axis=0, tiled=True)  27.7 us
    all_to_all x1, blocking collectives, on_device(): lax.all_to_all(block_rows, 'tok', split_axis=0, concat_axis=0, tiled=True)  17.2 us
    unnamed x25, local copies, waits for them, and re-layouts  16.1 us
    all_to_all x1, blocking collectives, on_device(): lax.all_to_all(block_cot, 'tok', split_axis=0, concat_axis=0, tiled=True)  12.8 us
  transfers between devices with their start and end apart: 7, of which 7 were waited for; matrix products, arithmetic and copies ran while one was open for 15% of the time, Pallas kernels for 0%

commit v1 on v0

--- a/solution.py
+++ b/solution.py
@@ -41,7 +41,7 @@
     width = w_gate.shape[1]
     documents = jnp.arange(experts * groups, dtype=jnp.int32)
     doc_onehot = (segment_ids[:, None] == documents[None, :]).astype(jnp.float32)
-    doc_len = lax.psum(jnp.sum(doc_onehot, axis=0), ("tok", "grp"))
+    doc_len = jnp.sum(lax.all_gather(jnp.sum(doc_onehot, axis=0), ("tok", "grp")), axis=0)
     tok_len = jnp.sum(doc_onehot * doc_len[None, :], axis=1)
     tok_weight = rows_here / tok_len
     onehot = (

time: 379 us -> 379 us (level)
  waiting for transfers between devices: 193 us -> 188 us
    unnamed x0 -> x1, blocking collectives: none -> 32.6 us
    psum x1 -> x0, blocking collectives: 32.2 us -> none  [on_device(): doc_len = lax.psum(jnp.sum(doc_onehot, axis=0), ('tok', 'grp'))]
    all_gather x1, waiting for transfers between devices: 10.2 us -> 5.28 us  [on_device(): lax.all_gather(came_rows, 'tp', axis=2, tiled=True)]
    unnamed x25 -> x28, local copies, waits for them, and re-layouts: 16.1 us -> 17.6 us
where the time goes in v1:
time: 379 us
  waiting for transfers between devices  188 us (50%)
  blocking collectives  99.2 us (26%)
  matrix products  43.9 us (12%)
  local copies, waits for them, and re-layouts  18.3 us (5%)
  between operations  14.9 us (4%)
  other arithmetic  7.45 us (2%)
  starting transfers between devices  6.88 us (2%)
    unnamed x7, waiting for transfers between devices  80.1 us
    all_gather x1, waiting for transfers between devices, on_device(): lax.all_gather(came_cot, 'tp', axis=2, tiled=True)  62.4 us
    psum x1, blocking collectives, on_device(): squares = lax.psum(jnp.sum(wide_hidden * wide_hidden, axis=1), 'tp')  34.2 us
    unnamed x1, blocking collectives  32.6 us
    all_gather x1, waiting for transfers between devices, on_device(): lax.all_gather(part_rows, 'grp', axis=0, tiled=True)  27.7 us
    unnamed x28, local copies, waits for them, and re-layouts  17.6 us
    all_to_all x1, blocking collectives, on_device(): lax.all_to_all(block_rows, 'tok', split_axis=0, concat_axis=0, tiled=True)  17.2 us
    all_to_all x1, blocking collectives, on_device(): lax.all_to_all(block_cot, 'tok', split_axis=0, concat_axis=0, tiled=True)  15.1 us
  transfers between devices with their start and end apart: 7, of which 7 were waited for; matrix products, arithmetic and copies ran while one was open for 15% of the time, Pallas kernels for 0%

profile of v1, /device:TPU:1, one launch (start us, length us, event | category | flops | bytes accessed | tf_op | source)
XLA Modules:
  0.0 378.6 jit_solution(10056331473833084322)
XLA Ops:
  9.5 34.2 %psum.7 = f32[128]{0:T(128)S(1)} all-reduce(f32[128]{0:T(128)S(1)} %fusion.19), channel_id=1, replica_groups=mesh['tok'=8,'tp'=16,'grp'=2] {'tp'}, use_global_device_ids=true, to_apply=%region_6.7 | all-reduce | flops 128 | bytes 1024 | tf_op jit(solution)/shard_map/psum | solution.py:60
  46.3 1.2 convolution_convert_fusion.1
  47.5 17.2 %all_to_all.15 = bf16[8,40,384]{2,1,0:T(8,128)(2,1)} all-to-all(bf16[8,40,384]{2,1,0:T(8,128)(2,1)S(1)} %bitcast.57), channel_id=1, replica_groups=mesh['tok'=8,'tp'=16,'grp'=2] {'tok'}, dimensions={0} | all-to-all | bytes 491520 | tf_op jit(solution)/shard_map/all_to_all | solution.py:70
  64.8 1.3 dynamic-slice
  67.7 32.6 %all-reduce = f32[256]{0:T(256)S(1)} all-reduce(f32[256]{0:T(256)S(1)} %dynamic-update-slice), channel_id=2, replica_groups=mesh['tok'=8,'tp'=16,'grp'=2] {'tok','grp'}, use_global_device_ids=true, to_apply=%add | all-reduce | flops 256 | bytes 2048
  101.9 1.5 select_reduce_fusion
  103.6 15.1 %all_to_all.16 = bf16[8,40,384]{2,1,0:T(8,128)(2,1)} all-to-all(bf16[8,40,384]{2,1,0:T(8,128)(2,1)S(1)} %bitcast.58), channel_id=1, replica_groups=mesh['tok'=8,'tp'=16,'grp'=2] {'tok'}, dimensions={0} | all-to-all | bytes 491520 | tf_op jit(solution)/shard_map/all_to_all | solution.py:71
  118.8 5.3 %all-gather.6.cloned.1.call-done = bf16[8,40,6144]{2,1,0:T(8,128)(2,1)} async-done(((bf16[8,40,384]{2,1,0:T(8,128)(2,1)}), bf16[8,40,6144]{2,1,0:T(8,128)(2,1)}) %all-gather.6.cloned.1.call-update) | async-done | bytes 3932176 | tf_op jit(solution)/shard_map/all_gather | solution.py:74
  124.1 62.4 %all-gather.10.cloned.1.call-done = bf16[8,40,6144]{2,1,0:T(8,128)(2,1)} async-done(((bf16[8,40,384]{2,1,0:T(8,128)(2,1)}), bf16[8,40,6144]{2,1,0:T(8,128)(2,1)}) %all-gather.10.cloned.1.call-update) | async-done | bytes 3932176 | tf_op jit(solution)/shard_map/all_gather | solution.py:75
  186.5 27.7 %all-gather.8.cloned.1.call-done = bf16[16,40,6144]{2,1,0:T(8,128)(2,1)} async-done(((bf16[8,40,6144]{2,1,0:T(8,128)(2,1)}), bf16[16,40,6144]{2,1,0:T(8,128)(2,1)}) %all-gather.8.cloned.1.call-update) | async-done | bytes 7864336 | tf_op jit(solution)/shard_map/all_gather | solution.py:78
  214.2 5.6 %fusion.9 = f32[640,256]{1,0:T(8,128)S(1)} fusion(bf16[640,6144]{1,0:T(8,128)(2,1)} %bitcast.61, bf16[1,6144,256]{2,1,0:T(8,128)(2,1)S(1)} %copy-done.4), kind=kOutput, calls=%fused_computation.13 | convolution fusion | flops 2013265920 | bytes 11665408 | tf_op jit(solution)/shard_map/dot_general | solution.py:8
  220.6 3.0 multiply_convert_fusion.2
  224.4 6.1 %fusion = bf16[6144,640]{0,1:T(8,128)(2,1)} fusion(bf16[640,256]{1,0:T(8,128)(2,1)S(1)} %get-tuple-element.4, bf16[1,256,6144]{2,1,0:T(8,128)(2,1)S(1)} %copy-done.1), kind=kOutput, calls=%fused_computation.1 | convolution fusion | flops 2017198080 | bytes 11337728 | tf_op jit(solution)/shard_map/dot_general | solution.py:89
  230.5 10.7 %copy.34 = bf16[6144,640]{1,0:T(8,128)(2,1)} copy(bf16[6144,640]{0,1:T(8,128)(2,1)} %fusion) | data formatting | bytes 15728640
  241.6 5.6 %fusion.4 = f32[640,256]{1,0:T(8,128)S(1)} fusion(bf16[640,6144]{1,0:T(8,128)(2,1)} %bitcast.54, bf16[1,256,6144]{2,1,0:T(8,128)(2,1)S(1)} %copy-done.1), kind=kOutput, calls=%fused_computation.8 | convolution fusion | flops 2013265920 | bytes 11665408 | tf_op jit(solution)/shard_map/dot_general | solution.py:13
  248.1 6.2 %fusion.11 = f32[256]{0:T(256)S(1)} fusion(bf16[1,6144,256]{2,1,0:T(8,128)(2,1)S(1)} %copy-done.5, bf16[640,6144]{1,0:T(8,128)(2,1)} %bitcast.62, f32[640,256]{1,0:T(8,128)S(1)} %copy-done.8, f32[640,256]{1,0:T(8,128)S(1)} %fusion.4, f32[640,256]{1,0:T(8,128)S(1)} %copy-done.10), kind=kOutput, calls=%fused_computation.15 | convolution fusion | flops 2021195520 | bytes 12977152 | tf_op jit(solution)/shard_map/dot_general | solution.py:20
  254.3 80.0 %reduce-scatter.7.cloned.1.call-done = bf16[384,640]{1,0:T(8,128)(2,1)} async-done(((bf16[6144,640]{1,0:T(8,128)(2,1)}), bf16[384,640]{1,0:T(8,128)(2,1)}) %reduce-scatter.7.cloned.1.call-update) | async-done | bytes 491536
  334.3 2.0 copy.35
  336.4 7.4 %fusion.12 = f32[256]{0:T(256)S(1)} fusion(bf16[1,6144,256]{2,1,0:T(8,128)(2,1)} %param.16, bf16[640,6144]{1,0:T(8,128)(2,1)} %bitcast.63, f32[640,256]{1,0:T(8,128)} %copy-done.9, f32[640,256]{1,0:T(8,128)} %copy-done.7), kind=kOutput, calls=%fused_computation.16 | convolution fusion | flops 2020540160 | bytes 12321792 | tf_op jit(solution)/shard_map/dot_general | solution.py:23
  343.7 7.7 %reduce-scatter.5.cloned.1.call-done = bf16[384,320]{0,1:T(8,128)(2,1)} async-done(((bf16[384,640]{0,1:T(8,128)(2,1)}), bf16[384,320]{0,1:T(8,128)(2,1)}) %reduce-scatter.5.cloned.1.call-update) | async-done | bytes 245776 | tf_op jit(solution)/shard_map/reduce_scatter | solution.py:96
  351.4 6.5 %all-to-all-start.1 = ((bf16[384,8,40]{0,2,1:T(8,128)(2,1)}), bf16[384,8,40]{0,2,1:T(8,128)(2,1)S(1)}, u32[]{:S(2)}, u32[]{:S(2)}) async-start(bf16[384,8,40]{0,2,1:T(8,128)(2,1)} %bitcast.59), calls=%async_computation.2 | async-start | bytes 491520 | tf_op jit(solution)/shard_map/all_to_all | solution.py:101
  357.8 6.5 %fusion.13 = f32[256]{0:T(256)S(1)} fusion(bf16[1,256,6144]{2,1,0:T(8,128)(2,1)S(1)} %copy-done.1, bf16[640,256]{1,0:T(8,128)(2,1)} %copy-done.2, bf16[640,6144]{1,0:T(8,128)(2,1)} %bitcast.55), kind=kOutput, calls=%fused_computation.17 | convolution fusion | flops 2019557120 | bytes 11338752 | tf_op jit(solution)/shard_map/dot_general | solution.py:26
  364.9 4.8 %all-to-all-done.1 = bf16[384,8,40]{0,2,1:T(8,128)(2,1)S(1)} async-done(((bf16[384,8,40]{0,2,1:T(8,128)(2,1)}), bf16[384,8,40]{0,2,1:T(8,128)(2,1)S(1)}, u32[]{:S(2)}, u32[]{:S(2)}) %all-to-all-start.1) | async-done | bytes 245792 | tf_op jit(solution)/shard_map/all_to_all | solution.py:101
  369.7 2.0 fusion.15
  (61 shorter events, 11.2 us)
Async XLA Ops:
  7.2 96.2 %copy-start = (bf16[128,384]{1,0:T(8,128)(2,1)S(1)}, bf16[128,384]{1,0:T(8,128)(2,1)}, u32[]{:S(2)}) copy-start(bf16[128,384]{1,0:T(8,128)(2,1)} %param.14) | copy-start | bytes 294916
  7.2 207.0 %copy-start.4 = (bf16[1,6144,256]{2,1,0:T(8,128)(2,1)S(1)}, bf16[1,6144,256]{2,1,0:T(8,128)(2,1)}, u32[]{:S(2)}) copy-start(bf16[1,6144,256]{2,1,0:T(8,128)(2,1)} %param.15) | copy-start | bytes 9437188
  7.2 116.8 %all-gather.6.cloned.1.call-start = ((), (), s32[]{:S(2)}) async-start(), calls=%async_computation.5 | async-start | bytes 4177920 | tf_op jit(solution)/shard_map/all_gather | solution.py:74
  64.7 121.7 %all-gather.10.cloned.1.call-start = ((), (), s32[]{:S(2)}) async-start(), calls=%async_computation.8 | async-start | bytes 4177920 | tf_op jit(solution)/shard_map/all_gather | solution.py:75
  118.7 95.5 %all-gather.8.cloned.1.call-start = ((), (), s32[]{:S(2)}) async-start(), calls=%async_computation.6 | async-start | bytes 11796480 | tf_op jit(solution)/shard_map/all_gather | solution.py:78
  124.1 117.6 %all-gather.12.cloned.1.call-start = ((), (), s32[]{:S(2)}) async-start(), calls=%async_computation.9 | async-start | bytes 11796480 | tf_op jit(solution)/shard_map/all_gather | solution.py:79
  186.5 147.8 %reduce-scatter.7.cloned.1.call-start = ((), (), s32[]{:S(2)}) async-start(), calls=%async_computation.10 | async-start | bytes 8355840
  214.2 5.6 %copy-start.3 = (bf16[16,40,6144]{2,1,0:T(8,128)(2,1)S(1)}, bf16[16,40,6144]{2,1,0:T(8,128)(2,1)}, u32[]{:S(2)}) copy-start(bf16[16,40,6144]{2,1,0:T(8,128)(2,1)} %all-gather.8.cloned.1.call-done) | copy-start | bytes 23592964
  214.2 6.4 %copy-start.6 = (bf16[1,6144,256]{2,1,0:T(8,128)(2,1)S(1)}, bf16[1,6144,256]{2,1,0:T(8,128)(2,1)}, u32[]{:S(2)}) copy-start(bf16[1,6144,256]{2,1,0:T(8,128)(2,1)} %param.16) | copy-start | bytes 9437188
  220.6 3.0 copy-start.7
  220.6 3.8 copy-start.1
  223.6 0.7 copy-start.2
  241.2 110.1 %reduce-scatter.5.cloned.1.call-start = ((), (), s32[]{:S(2)}) async-start(), calls=%async_computation.7 | async-start | bytes 737280 | tf_op jit(solution)/shard_map/reduce_scatter | solution.py:96
  241.6 6.5 %copy-start.5 = (bf16[1,6144,256]{2,1,0:T(8,128)(2,1)S(1)}, bf16[1,6144,256]{2,1,0:T(8,128)(2,1)}, u32[]{:S(2)}) copy-start(bf16[1,6144,256]{2,1,0:T(8,128)(2,1)} %param.15) | copy-start | bytes 9437188
  241.6 6.5 %copy-start.8 = (f32[640,256]{1,0:T(8,128)S(1)}, f32[640,256]{1,0:T(8,128)}, u32[]{:S(2)}) copy-start(f32[640,256]{1,0:T(8,128)} %copy-done.7) | copy-start | bytes 1966084
  241.6 6.5 %copy-start.10 = (f32[640,256]{1,0:T(8,128)S(1)}, f32[640,256]{1,0:T(8,128)}, u32[]{:S(2)}) copy-start(f32[640,256]{1,0:T(8,128)} %get-tuple-element.5) | copy-start | bytes 1966084
  247.2 0.8 copy-start.9
  351.4 18.3 %all-to-all-start.1 = ((bf16[384,8,40]{0,2,1:T(8,128)(2,1)}), bf16[384,8,40]{0,2,1:T(8,128)(2,1)S(1)}, u32[]{:S(2)}, u32[]{:S(2)}) async-start(bf16[384,8,40]{0,2,1:T(8,128)(2,1)} %bitcast.59), calls=%async_computation.2 | async-start | bytes 491520 | tf_op jit(solution)/shard_map/all_to_all | solution.py:101
Sparse Core Ops, SparseCore 0:
  64.9 59.1 all-gather.5
  126.4 59.9 all-gather.9
  188.3 25.9 all-gather.7
  215.9 25.6 all-gather.11
  245.3 89.0 reduce-scatter.6
  336.7 14.6 reduce-scatter.4
